TPU v7x, 256 devices: a whole 4x4x8 slice. The times are simulated.
256 devices in a mesh: item: 64 (over z, y, core), dp: 4 (over x).
Axes of the slice: x: 4, y: 4, z: 8, core: 2. Of those that a mesh axis runs over, the one named last changes fastest.
Arguments:
- query_feats: bfloat16 [4, 1024, 256], P('dp', 'item'), may hold values from -6 to 6
- positives: int32 [4, 1024], P('dp'), may hold values from 0 to 262143
- query_count: int32 [4, 64], P('dp'), may hold values from 1 to 16, as said below
- item_table: bfloat16 [262144, 256], P('item'), may hold values from -6 to 6
- item_gates: float32 [4, 262144], P(None, 'item'), may hold values from -5 to 5
- w_in: bfloat16 [256, 512], replicated, may hold values from -0.375 to 0.375
- w_out: bfloat16 [512, 256], replicated, may hold values from -0.25 to 0.25
- w_gate: bfloat16 [512, 4], replicated, may hold values from -1.25 to 1.25
Outputs:
- grad_feats: float32 [4, 1024, 256], P('dp', 'item')
- grad_w_in: float32 [256, 512], replicated
- grad_w_out: float32 [512, 256], replicated
- grad_w_gate: float32 [512, 4], replicated
Inputs may be any that keep to these rules, and one draw needn't show every extreme that they name: `query_count`: valid queries of a device's slots; the counts of one group sum to at most 768, exactly that in some group, and some device of every group has all 16 slots valid.
All inputs are finite; a program needn't handle non-finite values.
Results may differ from a plain program's by a relative error of at most 0.0053.
Values may be sent and summed in bfloat16 or wider, within the bound.
A program may use at most 64 MiB of HBM per device.

v0:
```python
import jax
import jax.numpy as jnp
from jax import lax
from jax.sharding import PartitionSpec as P

EPS = 1e-06
TAU = 0.05


def unit_rows(raw_vals):
    scale = lax.rsqrt(jnp.sum(raw_vals * raw_vals, axis=-1, keepdims=True) + EPS)
    return (raw_vals * scale, scale)


def gate_weights(gate_logits, reduce_axis):
    exp_terms = jnp.exp(gate_logits)
    return exp_terms / jnp.sum(exp_terms, axis=reduce_axis, keepdims=True)


def item_sweep(query_rows, query_gate, item_norm, item_gates):
    row_count = query_rows.shape[0]
    components = query_rows.shape[1]
    comp_width = query_rows.shape[2]
    item_span = item_norm.shape[0]
    block_len = min(512, item_span)
    block_count = item_span // block_len
    item_blocks = item_norm.reshape(block_count, block_len, components, comp_width)
    gate_blocks = item_gates.reshape(components, block_count, block_len).transpose(1, 0, 2)
    gate_f = query_gate.astype(jnp.float32).T[:, :, None]

    def one_block(state_in, input_block_part):
        totals, update_delta, gate_sum = state_in
        item_part, gate_part = input_block_part
        score_matrix = jnp.einsum(
            "rkd,ikd->kri", query_rows, item_part, preferred_element_type=jnp.float32
        )
        weights = gate_weights(gate_f + gate_part[:, None, :], 0)
        logits = jnp.sum(weights * score_matrix, axis=0) / TAU
        exp_logit = jnp.exp(logits)
        totals = totals + jnp.sum(exp_logit, axis=1)
        coef_bf = (exp_logit[None] * weights / TAU).astype(jnp.bfloat16)
        update_delta = update_delta + jnp.einsum(
            "kri,ikd->rkd", coef_bf, item_part, preferred_element_type=jnp.float32
        )
        gate_sum = (
            gate_sum
            + jnp.sum(exp_logit[None] * weights * (score_matrix - TAU * logits[None]), axis=2) / TAU
        )
        return ((totals, update_delta, gate_sum), None)

    initial = (
        jnp.zeros((row_count,), jnp.float32),
        jnp.zeros((row_count, components, comp_width), jnp.float32),
        jnp.zeros((components, row_count), jnp.float32),
    )
    (totals, update_delta, gate_sum), _ = lax.scan(one_block, initial, (item_blocks, gate_blocks))
    return (totals, update_delta, gate_sum.T)


def positive_terms(query_rows, query_gate, positive, item_norm, item_gates, item_base):
    item_span = item_norm.shape[0]
    local_id = positive - item_base
    inside = (local_id >= 0) & (local_id < item_span)
    safe_id = jnp.clip(local_id, 0, item_span - 1)
    item_pos = jnp.take(item_norm, safe_id, axis=0).astype(jnp.float32)
    gate_pos = jnp.take(item_gates, safe_id, axis=1).T
    query_float_rows = query_rows.astype(jnp.float32)
    score_pos = jnp.sum(query_float_rows * item_pos, axis=-1)
    weight_pos = gate_weights(query_gate.astype(jnp.float32) + gate_pos, 1)
    logit_pos = jnp.sum(weight_pos * score_pos, axis=-1) / TAU
    keep_rows = inside.astype(jnp.float32)
    pos_query = weight_pos[:, :, None] * item_pos / TAU * keep_rows[:, None, None]
    pos_gate = weight_pos * (score_pos - TAU * logit_pos[:, None]) / TAU * keep_rows[:, None]
    return (pos_query, pos_gate)


def per_device(query_feats, positives, query_count, item_table, item_gates, w_in, w_out, w_gate):
    shard_count = lax.axis_size("item")
    item_rank = lax.axis_index("item")
    own_rows = query_feats.shape[1]
    feat_width = query_feats.shape[2]
    components = w_gate.shape[1]
    emb_width = w_out.shape[1]
    comp_width = emb_width // components
    slot_total = own_rows * shard_count
    features = query_feats[0]
    counts = query_count[0]
    preact = jnp.dot(features, w_in, preferred_element_type=jnp.float32)
    hidden = jax.nn.silu(preact).astype(jnp.bfloat16)
    query_raw = jnp.dot(hidden, w_out, preferred_element_type=jnp.float32).reshape(
        own_rows, components, comp_width
    )
    query_gate = jnp.dot(hidden, w_gate, preferred_element_type=jnp.float32).astype(jnp.bfloat16)
    query_unit, query_scale = unit_rows(query_raw)
    query_norm = query_unit.astype(jnp.bfloat16).reshape(own_rows, emb_width)
    all_query, all_gate = (
        lax.all_gather(query_norm, "item", axis=0, tiled=True),
        lax.all_gather(query_gate, "item", axis=0, tiled=True),
    )
    item_span = item_table.shape[0]
    item_norm = unit_rows(
        item_table.astype(jnp.float32).reshape(item_span, components, comp_width)
    )[0].astype(jnp.bfloat16)
    slot_in_dev = jnp.arange(own_rows, dtype=jnp.int32)
    valid_slot = (slot_in_dev[None, :] < counts[:, None]).reshape(slot_total)
    item_base = item_rank * item_span
    group_position = positives[0]
    query_rows = all_query.reshape(-1, components, comp_width)
    totals, update_delta, gate_sum = item_sweep(query_rows, all_gate, item_norm, item_gates)
    pos_query, pos_gate = positive_terms(
        query_rows, all_gate, group_position, item_norm, item_gates, item_base
    )
    live_f = valid_slot.astype(jnp.float32)
    totals_all = lax.psum(totals, "item")
    query_term_part = (update_delta / totals_all[:, None, None] - pos_query) * live_f[:, None, None]
    term_gate = (gate_sum / totals_all[:, None] - pos_gate) * live_f[:, None]
    grad_query, grad_gate = (
        lax.psum_scatter(
            query_term_part.reshape(slot_total, emb_width), "item", scatter_dimension=0, tiled=True
        ),
        lax.psum_scatter(term_gate, "item", scatter_dimension=0, tiled=True),
    )
    grad_query = grad_query.reshape(own_rows, components, comp_width)
    dot_sum = jnp.sum(grad_query * query_raw, axis=-1, keepdims=True)
    grad_raw = (query_scale * grad_query - query_raw * query_scale**3 * dot_sum).reshape(
        own_rows, emb_width
    )
    highest = lax.Precision.HIGHEST
    grad_hidden = jnp.dot(grad_raw, w_out.astype(jnp.float32).T, precision=highest) + jnp.dot(
        grad_gate, w_gate.astype(jnp.float32).T, precision=highest
    )
    sigmoid_pre = jax.nn.sigmoid(preact)
    grad_preact = grad_hidden * sigmoid_pre * (1.0 + preact * (1.0 - sigmoid_pre))
    grad_feats = jnp.dot(grad_preact, w_in.astype(jnp.float32).T, precision=highest).reshape(
        1, own_rows, feat_width
    )
    hidden_f = hidden.astype(jnp.float32)
    part_in = jnp.dot(features.astype(jnp.float32).T, grad_preact, precision=highest)
    part_out = jnp.dot(hidden_f.T, grad_raw, precision=highest)
    part_gate = jnp.dot(hidden_f.T, grad_gate, precision=highest)
    grad_w_in, grad_w_out, grad_w_gate = lax.psum((part_in, part_out, part_gate), ("item", "dp"))
    return (grad_feats, grad_w_in, grad_w_out, grad_w_gate)


def solution(mesh):
    in_specs = (
        P("dp", "item", None),
        P("dp", None),
        P("dp", None),
        P("item", None),
        P(None, "item"),
        P(),
        P(),
        P(),
    )
    out_specs = (P("dp", "item", None), P(), P(), P())
    return jax.shard_map(
        per_device, mesh=mesh, in_specs=in_specs, out_specs=out_specs, check_vma=False
    )
```

profile of v0, /device:TPU:2, one launch (start us, length us, event | category | flops | bytes accessed | tf_op | source)
XLA Modules:
  0.0 914.7 jit_solution(16929554966947675786)
XLA Ops:
  16.9 53.5 %all_gather.7 = bf16[1024,256]{1,0:T(8,128)(2,1)S(1)} all-gather(bf16[16,256]{1,0:T(8,128)(2,1)S(1)} %multiply_convert_fusion.9), channel_id=1, replica_groups=mesh['item'=64,'dp'=4] {'item'}, dimensions={0}, use_global_device_ids=true | all-gather | bytes 532480 | tf_op jit(solution)/shard_map/all_gather | solution.py:97
  73.4 7.0 copy.75
  80.4 5.7 gather_fusion.1
  87.5 42.9 %all-gather = bf16[64,16,4]{1,2,0:T(4,128)(2,1)S(1)} all-gather(bf16[1,16,4]{1,2,0:T(4,128)(2,1)S(1)} %fusion.19), channel_id=1, replica_groups=mesh['item'=64,'dp'=4] {'item'}, dimensions={0}, use_global_device_ids=true | all-gather | bytes 8320 | tf_op jit(solution)/shard_map/all_gather | solution.py:98
  132.1 4.4 gather_fusion
  137.7 6.0 copy.81
  147.2 118.4 %while.17 = (s32[]{:T(128)}, f32[1024]{0:T(1024)S(1)}, f32[1024,4,64]{0,2,1:T(8,128)}, f32[4,1024]{1,0:T(4,128)S(1)}, f32[4,1024,1]{1,0,2:T(4,128)S(1)}, /*index...) while((s32[]{:T(128)}, f32[1024]{0:T(1024)S(1)}, ...), condition=%wide.region_7.8_spmd.clone, body=%wide.region_2.7_spmd.clone.sunk | while | flops 573056000 | bytes 49480844 | solution.py:56
  149.4 4.1 fusion.63
  153.8 3.0 fusion.65
  156.8 5.0 fusion.64
  164.0 4.1 fusion.63
  168.4 3.0 fusion.65
  171.4 5.3 fusion.64
  178.8 4.1 fusion.63
  183.2 3.0 fusion.65
  186.2 5.3 fusion.64
  193.6 4.1 fusion.63
  198.0 3.0 fusion.65
  201.1 5.3 fusion.64
  208.4 4.1 fusion.63
  212.9 3.0 fusion.65
  215.9 5.3 fusion.64
  223.3 4.1 fusion.63
  230.7 5.3 fusion.64
  238.1 4.1 fusion.63
  245.5 5.3 fusion.64
  252.9 4.1 fusion.63
  260.4 5.3 fusion.64
  265.7 126.8 %psum.28 = f32[1024]{0:T(1024)S(1)} all-reduce(f32[1024]{0:T(1024)S(1)} %get-tuple-element.108), channel_id=1, replica_groups=mesh['item'=64,'dp'=4] {'item'}, use_global_device_ids=true, to_apply=%region_8.9 | all-reduce | flops 1024 | bytes 8192 | tf_op jit(solution)/shard_map/psum | solution.py:114
  398.0 249.1 %all-reduce = f32[1024,4]{1,0:T(8,128)S(1)} all-reduce(f32[1024,4]{1,0:T(8,128)S(1)} %copy.78), channel_id=3, replica_groups=mesh['item'=64,'dp'=4] {'item'}, use_global_device_ids=true, to_apply=%region_14.15.clone | all-reduce | flops 4096 | bytes 32768
  652.1 71.6 %psum.31 = f32[512,4]{0,1:T(4,128)} all-reduce(f32[512,4]{0,1:T(4,128)S(1)} %fusion.30), channel_id=1, replica_groups=mesh['item'=64,'dp'=4] {'item','dp'}, use_global_device_ids=true, to_apply=%region_17.18 | all-reduce | flops 2048 | bytes 16384 | tf_op jit(solution)/shard_map/psum | solution.py:141
  724.6 179.4 %all-reduce.4.cloned.1.call-done = (f32[256,512]{0,1:T(8,128)}, f32[512,256]{1,0:T(8,128)}) async-done(((f32[256,512]{0,1:T(8,128)}, f32[512,256]{1,0:T(8,128)}), (f32[256,512]{0,1:T(8,128)}, f32[512,256]{1,0:T(8,128)})) %all-reduce.4.cloned.1.call-update) | async-done | bytes 1048592 | tf_op jit(solution)/shard_map/psum | solution.py:141
  (161 shorter events, 63.8 us)
Async XLA Ops:
  7.2 7.3 copy-start
  7.2 639.9 %reduce-scatter.2.cloned.1.call-start = ((), (), s32[]{:S(2)}) async-start(), calls=%async_computation.1 | async-start | bytes 1064960 | tf_op jit(solution)/shard_map/reduce_scatter | solution.py:118
  10.2 3.6 copy-start.16
  10.2 4.2 copy-start.11
  10.2 5.0 copy-start.2
  16.3 0.6 copy-start.7
  73.4 13.9 %copy-start.18 = (bf16[512,4]{0,1:T(4,128)(2,1)S(1)}, bf16[512,4]{0,1:T(4,128)(2,1)}, u32[]{:S(2)}) copy-start(bf16[512,4]{0,1:T(4,128)(2,1)} %param.17) | copy-start | bytes 12292
  80.4 7.1 copy-start.10
  137.7 8.9 copy-start.5
  143.7 2.7 copy-start.15
  144.3 2.9 copy-start.4
  147.2 245.3 %copy-start.17 = (s32[1,64]{1,0:T(1,128)S(1)}, s32[1,64]{1,0:T(1,128)}, u32[]{:S(2)}) copy-start(s32[1,64]{1,0:T(1,128)} %param.12) | copy-start | bytes 772
  147.2 245.4 %copy-start.6 = (f32[1024,4]{0,1:T(4,128)S(1)}, f32[1024,4]{0,1:T(4,128)}, u32[]{:S(2)}) copy-start(f32[1024,4]{0,1:T(4,128)} %copy-done.5) | copy-start | bytes 49156
  149.4 4.4 copy-start.1
  163.9 4.4 copy-start.1
  178.8 4.4 copy-start.1
  193.6 4.4 copy-start.1
  208.4 4.4 copy-start.1
  223.3 4.4 copy-start.1
  238.1 4.4 copy-start.1
  252.9 4.4 copy-start.1
  265.6 130.7 %copy-start.9 = (f32[1,1024]{1,0:T(1,128)S(1)}, f32[1,1024]{1,0:T(1,128)}, u32[]{:S(2)}) copy-start(f32[1,1024]{1,0:T(1,128)} %and_select_fusion) | copy-start | bytes 12292
  265.6 130.9 %copy-start.14 = (f32[16,4]{1,0:T(8,128)S(1)}, f32[16,4]{1,0:T(8,128)}, u32[]{:S(2)}) copy-start(f32[16,4]{1,0:T(8,128)} %get-tuple-element.223) | copy-start | bytes 772
  265.7 131.1 %copy-start.20 = (u32[256]{0:T(256)S(1)}, u32[256]{0:T(256)}, u32[]{:S(2)}) copy-start(u32[256]{0:T(256)} %constant.108) | copy-start | bytes 3076
  265.7 382.5 %copy-start.8 = (f32[16,256]{1,0:T(8,128)S(1)}, f32[16,256]{1,0:T(8,128)}, u32[]{:S(2)}) copy-start(f32[16,256]{1,0:T(8,128)} %copy-done.7) | copy-start | bytes 49156
  265.7 383.3 %copy-start.3 = (bf16[512,256]{1,0:T(8,128)(2,1)S(1)}, bf16[512,256]{1,0:T(8,128)(2,1)}, u32[]{:S(2)}) copy-start(bf16[512,256]{1,0:T(8,128)(2,1)} %param.16) | copy-start | bytes 786436
  393.4 257.1 %copy-start.13 = (f32[16,512]{1,0:T(8,128)S(1)}, f32[16,512]{1,0:T(8,128)}, u32[]{:S(2)}) copy-start(f32[16,512]{1,0:T(8,128)} %get-tuple-element.226) | copy-start | bytes 98308
  393.4 257.1 %copy-start.19 = (bf16[512,4]{0,1:T(4,128)(2,1)S(1)}, bf16[512,4]{0,1:T(4,128)(2,1)}, u32[]{:S(2)}) copy-start(bf16[512,4]{0,1:T(4,128)(2,1)} %param.17) | copy-start | bytes 12292
  393.4 257.2 %copy-start.12 = (bf16[1,16,256]{2,1,0:T(8,128)(2,1)S(1)}, bf16[1,16,256]{2,1,0:T(8,128)(2,1)}, u32[]{:S(2)}) copy-start(bf16[1,16,256]{2,1,0:T(8,128)(2,1)} %param.10) | copy-start | bytes 24580
  396.2 507.7 %all-reduce.4.cloned.1.call-start = ((), (), s32[]{:S(2)}) async-start(), calls=%async_computation.2 | async-start | bytes 2097152 | tf_op jit(solution)/shard_map/psum | solution.py:141
Sparse Core Ops, SparseCore 0:
  396.4 134.9 reduce-scatter.1
  652.0 251.9 all-reduce.3
where the time goes:
time: 916 us; the launch traced here: 915 us
  blocking collectives  544 us (59%)
  waiting for transfers between devices  179 us (20%)
  matrix products  79.4 us (9%)
  other arithmetic  51.6 us (6%)
  local copies, waits for them, and re-layouts  45 us (5%)
  between operations  15 us (2%)
    unnamed x1, blocking collectives  249 us
    psum x1, waiting for transfers between devices, per_device(): lax.psum((part_in, part_out, part_gate), ('item', 'dp'))  179 us
    psum x1, blocking collectives, per_device(): totals_all = lax.psum(totals, 'item')  127 us
    psum x1, blocking collectives, per_device(): lax.psum((part_in, part_out, part_gate), ('item', 'dp'))  71.6 us
    all_gather x1, blocking collectives, per_device(): lax.all_gather(query_norm, 'item', axis=0, tiled=True)  53.5 us
    all_gather x1, blocking collectives, per_device(): lax.all_gather(query_gate, 'item', axis=0, tiled=True)  42.9 us
    dot_general x8, matrix products, one_block(): jnp.einsum('kri,ikd->rkd', coef_bf, item_part, preferred_element_type=jnp...  41.9 us
    dot_general x8, matrix products, one_block(): jnp.einsum('rkd,ikd->kri', query_rows, item_part, preferred_element_type=...  32.5 us
  transfers between devices with their start and end apart: 2, of which 1 were waited for; matrix products, arithmetic and copies ran while one was open for 0% of the time, Pallas kernels for 0%

commit v1 on v0

--- a/solution.py
+++ b/solution.py
@@ -138,7 +138,15 @@
     part_in = jnp.dot(features.astype(jnp.float32).T, grad_preact, precision=highest)
     part_out = jnp.dot(hidden_f.T, grad_raw, precision=highest)
     part_gate = jnp.dot(hidden_f.T, grad_gate, precision=highest)
-    grad_w_in, grad_w_out, grad_w_gate = lax.psum((part_in, part_out, part_gate), ("item", "dp"))
+
+    def _perform_frames(xin, mesh_name, bus_axis):
+        for to_i in (mesh_name, bus_axis):
+            xin = jax.lax.psum(xin, to_i)
+        return xin
+
+    grad_w_in, grad_w_out, grad_w_gate = _perform_frames(
+        (part_in, part_out, part_gate), "dp", "item"
+    )
     return (grad_feats, grad_w_in, grad_w_out, grad_w_gate)
 
 

time: 916 us -> 902 us (0.985)
  waiting for transfers between devices: 179 us -> 99.1 us
  blocking collectives: 544 us -> 610 us
    psum x1 -> x2, waiting for transfers between devices: 179 us -> 99 us  [_perform_frames(): xin = jax.lax.psum(xin, to_i)]
    psum x1 -> x2, blocking collectives: 71.6 us -> 138 us  [_perform_frames(): xin = jax.lax.psum(xin, to_i)]
  transfers between devices with their start and end apart: 2 -> 3, of which waited for: 1 -> 2; matrix products, arithmetic and copies ran while one was open for 0% -> 0% of each run, Pallas kernels for 0% -> 0%
where the time goes in v1:
time: 902 us; the launch traced here: 900 us
  blocking collectives  610 us (68%)
  waiting for transfers between devices  99.1 us (11%)
  matrix products  79.4 us (9%)
  other arithmetic  51.6 us (6%)
  local copies, waits for them, and re-layouts  45 us (5%)
  between operations  14.7 us (2%)
    unnamed x1, blocking collectives  249 us
    psum x2, blocking collectives, _perform_frames(): xin = jax.lax.psum(xin, to_i)  138 us
    psum x1, blocking collectives, per_device(): totals_all = lax.psum(totals, 'item')  127 us
    psum x2, waiting for transfers between devices, _perform_frames(): xin = jax.lax.psum(xin, to_i)  99 us
    all_gather x1, blocking collectives, per_device(): lax.all_gather(query_norm, 'item', axis=0, tiled=True)  53.5 us
    all_gather x1, blocking collectives, per_device(): lax.all_gather(query_gate, 'item', axis=0, tiled=True)  42.9 us
    dot_general x8, matrix products, one_block(): jnp.einsum('kri,ikd->rkd', coef_bf, item_part, preferred_element_type=jnp...  41.9 us
    dot_general x8, matrix products, one_block(): jnp.einsum('rkd,ikd->kri', query_rows, item_part, preferred_element_type=...  32.5 us
  transfers between devices with their start and end apart: 3, of which 2 were waited for; matrix products, arithmetic and copies ran while one was open for 0% of the time, Pallas kernels for 0%

profile of v1, /device:TPU:2, one launch (start us, length us, event | category | flops | bytes accessed | tf_op | source)
XLA Modules:
  0.0 900.2 jit_solution(4874927433128612118)
XLA Ops:
  16.9 53.5 %all_gather.7 = bf16[1024,256]{1,0:T(8,128)(2,1)S(1)} all-gather(bf16[16,256]{1,0:T(8,128)(2,1)S(1)} %multiply_convert_fusion.9), channel_id=1, replica_groups=mesh['item'=64,'dp'=4] {'item'}, dimensions={0}, use_global_device_ids=true | all-gather | bytes 532480 | tf_op jit(solution)/shard_map/all_gather | solution.py:97
  73.4 7.0 copy.75
  80.4 5.7 gather_fusion.1
  87.5 42.9 %all-gather = bf16[64,16,4]{1,2,0:T(4,128)(2,1)S(1)} all-gather(bf16[1,16,4]{1,2,0:T(4,128)(2,1)S(1)} %fusion.19), channel_id=1, replica_groups=mesh['item'=64,'dp'=4] {'item'}, dimensions={0}, use_global_device_ids=true | all-gather | bytes 8320 | tf_op jit(solution)/shard_map/all_gather | solution.py:98
  132.1 4.4 gather_fusion
  137.7 6.0 copy.81
  147.2 118.4 %while.17 = (s32[]{:T(128)}, f32[1024]{0:T(1024)S(1)}, f32[1024,4,64]{0,2,1:T(8,128)}, f32[4,1024]{1,0:T(4,128)S(1)}, f32[4,1024,1]{1,0,2:T(4,128)S(1)}, /*index...) while((s32[]{:T(128)}, f32[1024]{0:T(1024)S(1)}, ...), condition=%wide.region_7.8_spmd.clone, body=%wide.region_2.7_spmd.clone.sunk | while | flops 573056000 | bytes 49480844 | solution.py:56
  149.4 4.1 fusion.63
  153.8 3.0 fusion.65
  156.8 5.0 fusion.64
  164.0 4.1 fusion.63
  168.4 3.0 fusion.65
  171.4 5.3 fusion.64
  178.8 4.1 fusion.63
  183.2 3.0 fusion.65
  186.2 5.3 fusion.64
  193.6 4.1 fusion.63
  201.1 5.3 fusion.64
  208.4 4.1 fusion.63
  215.9 5.3 fusion.64
  223.3 4.1 fusion.63
  230.7 5.3 fusion.64
  238.1 4.1 fusion.63
  245.5 5.3 fusion.64
  252.9 4.1 fusion.63
  260.4 5.3 fusion.64
  265.7 126.8 %psum.49 = f32[1024]{0:T(1024)S(1)} all-reduce(f32[1024]{0:T(1024)S(1)} %get-tuple-element.108), channel_id=1, replica_groups=mesh['item'=64,'dp'=4] {'item'}, use_global_device_ids=true, to_apply=%region_8.9 | all-reduce | flops 1024 | bytes 8192 | tf_op jit(solution)/shard_map/psum | solution.py:114
  398.0 249.1 %all-reduce = f32[1024,4]{1,0:T(8,128)S(1)} all-reduce(f32[1024,4]{1,0:T(8,128)S(1)} %copy.78), channel_id=3, replica_groups=mesh['item'=64,'dp'=4] {'item'}, use_global_device_ids=true, to_apply=%region_14.15.clone | all-reduce | flops 4096 | bytes 32768
  651.9 45.9 %all-reduce.8.cloned.1.call-done = (f32[256,512]{0,1:T(8,128)}, f32[512,256]{1,0:T(8,128)}) async-done(((f32[256,512]{0,1:T(8,128)}, f32[512,256]{1,0:T(8,128)}), (f32[256,512]{0,1:T(8,128)}, f32[512,256]{1,0:T(8,128)})) %all-reduce.8.cloned.1.call-update) | async-done | bytes 1048592 | tf_op jit(solution)/shard_map/psum | solution.py:144
  698.0 9.1 %psum.54 = f32[512,4]{0,1:T(4,128)S(1)} all-reduce(f32[512,4]{0,1:T(4,128)S(1)} %fusion.30), channel_id=1, replica_groups=mesh['item'=64,'dp'=4] {'dp'}, use_global_device_ids=true, to_apply=%region_19.20 | all-reduce | flops 2048 | bytes 16384 | tf_op jit(solution)/shard_map/psum | solution.py:144
  707.2 128.5 %psum.55 = f32[512,4]{0,1:T(4,128)} all-reduce(f32[512,4]{0,1:T(4,128)S(1)} %psum.54), channel_id=1, replica_groups=mesh['item'=64,'dp'=4] {'item'}, use_global_device_ids=true, to_apply=%region_20.21 | all-reduce | flops 2048 | bytes 16384 | tf_op jit(solution)/shard_map/psum | solution.py:144
  836.6 53.1 %all-reduce.6.cloned.1.call-done = (f32[256,512]{0,1:T(8,128)}, f32[512,256]{1,0:T(8,128)}) async-done(((f32[256,512]{0,1:T(8,128)}, f32[512,256]{1,0:T(8,128)}), (f32[256,512]{0,1:T(8,128)}, f32[512,256]{1,0:T(8,128)})) %all-reduce.6.cloned.1.call-update) | async-done | bytes 1048592 | tf_op jit(solution)/shard_map/psum | solution.py:144
  (165 shorter events, 69.8 us)
Async XLA Ops:
  7.2 7.3 copy-start
  7.2 639.9 %reduce-scatter.2.cloned.1.call-start = ((), (), s32[]{:S(2)}) async-start(), calls=%async_computation.1 | async-start | bytes 1064960 | tf_op jit(solution)/shard_map/reduce_scatter | solution.py:118
  10.2 3.6 copy-start.16
  10.2 4.2 copy-start.11
  10.2 5.0 copy-start.2
  16.3 0.6 copy-start.7
  73.4 13.9 %copy-start.18 = (bf16[512,4]{0,1:T(4,128)(2,1)S(1)}, bf16[512,4]{0,1:T(4,128)(2,1)}, u32[]{:S(2)}) copy-start(bf16[512,4]{0,1:T(4,128)(2,1)} %param.17) | copy-start | bytes 12292
  80.4 7.1 copy-start.10
  137.7 8.9 copy-start.5
  143.7 2.7 copy-start.15
  144.3 2.9 copy-start.4
  147.2 245.3 %copy-start.17 = (s32[1,64]{1,0:T(1,128)S(1)}, s32[1,64]{1,0:T(1,128)}, u32[]{:S(2)}) copy-start(s32[1,64]{1,0:T(1,128)} %param.12) | copy-start | bytes 772
  147.2 245.4 %copy-start.6 = (f32[1024,4]{0,1:T(4,128)S(1)}, f32[1024,4]{0,1:T(4,128)}, u32[]{:S(2)}) copy-start(f32[1024,4]{0,1:T(4,128)} %copy-done.5) | copy-start | bytes 49156
  149.4 4.4 copy-start.1
  163.9 4.4 copy-start.1
  178.8 4.4 copy-start.1
  193.6 4.4 copy-start.1
  208.4 4.4 copy-start.1
  223.3 4.4 copy-start.1
  238.1 4.4 copy-start.1
  252.9 4.4 copy-start.1
  265.6 130.7 %copy-start.9 = (f32[1,1024]{1,0:T(1,128)S(1)}, f32[1,1024]{1,0:T(1,128)}, u32[]{:S(2)}) copy-start(f32[1,1024]{1,0:T(1,128)} %and_select_fusion) | copy-start | bytes 12292
  265.6 130.9 %copy-start.14 = (f32[16,4]{1,0:T(8,128)S(1)}, f32[16,4]{1,0:T(8,128)}, u32[]{:S(2)}) copy-start(f32[16,4]{1,0:T(8,128)} %get-tuple-element.225) | copy-start | bytes 772
  265.7 131.1 %copy-start.20 = (u32[256]{0:T(256)S(1)}, u32[256]{0:T(256)}, u32[]{:S(2)}) copy-start(u32[256]{0:T(256)} %constant.108) | copy-start | bytes 3076
  265.7 382.5 %copy-start.8 = (f32[16,256]{1,0:T(8,128)S(1)}, f32[16,256]{1,0:T(8,128)}, u32[]{:S(2)}) copy-start(f32[16,256]{1,0:T(8,128)} %copy-done.7) | copy-start | bytes 49156
  265.7 383.3 %copy-start.3 = (bf16[512,256]{1,0:T(8,128)(2,1)S(1)}, bf16[512,256]{1,0:T(8,128)(2,1)}, u32[]{:S(2)}) copy-start(bf16[512,256]{1,0:T(8,128)(2,1)} %param.16) | copy-start | bytes 786436
  393.4 257.1 %copy-start.13 = (f32[16,512]{1,0:T(8,128)S(1)}, f32[16,512]{1,0:T(8,128)}, u32[]{:S(2)}) copy-start(f32[16,512]{1,0:T(8,128)} %get-tuple-element.228) | copy-start | bytes 98308
  393.4 257.1 %copy-start.19 = (bf16[512,4]{0,1:T(4,128)(2,1)S(1)}, bf16[512,4]{0,1:T(4,128)(2,1)}, u32[]{:S(2)}) copy-start(bf16[512,4]{0,1:T(4,128)(2,1)} %param.17) | copy-start | bytes 12292
  393.4 257.2 %copy-start.12 = (bf16[1,16,256]{2,1,0:T(8,128)(2,1)S(1)}, bf16[1,16,256]{2,1,0:T(8,128)(2,1)}, u32[]{:S(2)}) copy-start(bf16[1,16,256]{2,1,0:T(8,128)(2,1)} %param.10) | copy-start | bytes 24580
  396.2 301.5 %all-reduce.8.cloned.1.call-start = ((), (), s32[]{:S(2)}) async-start(), calls=%async_computation.3 | async-start | bytes 2097152 | tf_op jit(solution)/shard_map/psum | solution.py:144
  651.9 237.9 %all-reduce.6.cloned.1.call-start = ((), (), s32[]{:S(2)}) async-start(), calls=%async_computation.2 | async-start | bytes 2097152 | tf_op jit(solution)/shard_map/psum | solution.py:144
Sparse Core Ops, SparseCore 0:
  396.4 134.9 reduce-scatter.1
  652.0 45.7 all-reduce.7
  701.7 188.0 all-reduce.5
